TPU v7x, 32 devices: a whole 2x2x4 slice. The times are simulated.
32 devices in a mesh: dp: 8 (over z, y), mp: 4 (over x, core).
Axes of the slice: x: 2, y: 2, z: 4, core: 2. Of those that a mesh axis runs over, the one named last changes fastest.
Arguments:
- query_inputs: bfloat16 [128, 28672], P(None, 'mp'), may hold values from -0.09375 to 0.09375
- query_grads: bfloat16 [128, 8192], P(None, 'mp'), may hold values from -6 to 6
- basis_inputs: bfloat16 [28672, 28672], P('mp', 'dp'), may hold values from -0.03125 to 0.03125
- basis_grads: bfloat16 [8192, 8192], P('mp', 'dp'), may hold values from -0.0625 to 0.0625
- eig_inputs: float32 [28672], P('dp'), may hold values from 0.25 to 4
- eig_grads: float32 [8192], P('dp'), may hold values from 0.25 to 4
- train_inputs: bfloat16 [6144, 28672], P('dp', 'mp'), may hold values from -0.03540039 to 0.03540039
- train_grads: bfloat16 [6144, 8192], P('dp', 'mp'), may hold values from -0.06591797 to 0.06591797
Outputs:
- scores: float32 [4, 48], P('mp', 'dp')
All inputs are finite; a program needn't handle non-finite values.
Results may differ from a plain program's by a relative error of at most 0.0054.
Values may be sent and summed in bfloat16 or wider, within the bound.
A program may use at most 128 MiB of HBM per device.

v0:
```python
import jax
import jax.numpy as jnp
from jax import lax
from jax.sharding import PartitionSpec as P

LEN = 128
QLEN = 32


def per_device(
    query_inputs,
    query_grads,
    basis_inputs,
    basis_grads,
    eig_inputs,
    eig_grads,
    train_inputs,
    train_grads,
):
    input_cols = basis_inputs.shape[1]
    feat_in = basis_inputs.shape[0]
    row_count = query_inputs.shape[0] // lax.axis_size("mp")
    rot_in = jnp.dot(query_inputs, basis_inputs, preferred_element_type=jnp.float32)
    rot_out = jnp.dot(query_grads, basis_grads, preferred_element_type=jnp.float32)
    rotated = lax.psum_scatter(
        jnp.concatenate([rot_in, rot_out], axis=1), "mp", scatter_dimension=0, tiled=True
    )
    scaled = jnp.concatenate(
        [
            rotated[:, :input_cols] / eig_inputs[None, :],
            rotated[:, input_cols:] / eig_grads[None, :],
        ],
        axis=1,
    ).astype(jnp.bfloat16)
    segment = lax.all_gather(scaled, "mp", axis=0, tiled=True)
    back_in = jnp.einsum(
        "qc,fc->qf", segment[:, :input_cols], basis_inputs, preferred_element_type=jnp.float32
    )
    back_out = jnp.einsum(
        "qc,fc->qf", segment[:, input_cols:], basis_grads, preferred_element_type=jnp.float32
    )
    partial_value = jnp.concatenate([back_in, back_out], axis=1)
    shared_part = lax.psum_scatter(partial_value, "dp", scatter_dimension=0, tiled=True).astype(
        jnp.bfloat16
    )
    directions = lax.all_gather(shared_part, "dp", axis=0, tiled=True)
    train_count = train_inputs.shape[0]
    inner_in = jnp.einsum(
        "qf,tf->qt", directions[:, :feat_in], train_inputs, preferred_element_type=jnp.float32
    )
    inner_out = jnp.einsum(
        "qf,tf->qt", directions[:, feat_in:], train_grads, preferred_element_type=jnp.float32
    )
    pair_sums = lax.psum_scatter(
        jnp.concatenate([inner_in, inner_out], axis=1), "mp", scatter_dimension=0, tiled=True
    )
    products = pair_sums[:, :train_count] * pair_sums[:, train_count:]
    grouped = products.reshape(row_count // QLEN, QLEN, train_count // LEN, LEN)
    return jnp.sum(grouped, axis=(1, 3))


def solution(mesh):
    return jax.shard_map(
        per_device,
        mesh=mesh,
        in_specs=(
            P(None, "mp"),
            P(None, "mp"),
            P("mp", "dp"),
            P("mp", "dp"),
            P("dp"),
            P("dp"),
            P("dp", "mp"),
            P("dp", "mp"),
        ),
        out_specs=P("mp", "dp"),
        check_vma=False,
    )
```

profile of v0, /device:TPU:0, one launch (start us, length us, event | category | flops | bytes accessed | tf_op | source)
XLA Modules:
  0.0 314.6 jit_solution(5288105056165067332)
XLA Ops:
  6.5 0.0 copy-start
  6.5 0.0 reduce-scatter.4.cloned.1.call-start
  6.5 4.0 %fusion.12 = f32[128,1024]{1,0:T(8,128)} fusion(bf16[128,2048]{1,0:T(8,128)(2,1)} %param.9, bf16[2048,1024]{1,0:T(8,128)(2,1)} %param.11), kind=kOutput, calls=%fused_computation.20 | convolution fusion | flops 536870912 | bytes 5242880 | tf_op jit(solution)/shard_map/dot_general | solution.py:24
  10.6 20.9 %fusion.11 = f32[128,3584]{1,0:T(8,128)} fusion(bf16[128,7168]{1,0:T(8,128)(2,1)} %param.8, bf16[7168,3584]{1,0:T(8,128)(2,1)} %param.10), kind=kOutput, calls=%fused_computation.19 | convolution fusion | flops 6576668672 | bytes 55050240 | tf_op jit(solution)/shard_map/dot_general | solution.py:23
  31.5 0.0 copy-start.3
  31.5 0.0 copy-start.2
  31.5 3.3 %pad_maximum_fusion.1 = f32[128,4608]{1,0:T(8,128)} fusion(f32[128,1024]{1,0:T(8,128)} %fusion.12, f32[128,3584]{1,0:T(8,128)} %fusion.11), kind=kLoop, calls=%fused_computation.1 | loop fusion | flops 589824 | bytes 4718592 | tf_op jit(solution)/shard_map/concatenate | solution.py:26
  34.7 0.0 reduce-scatter.4.cloned.1.call-update
  34.8 0.0 all-gather.3.cloned.1.call-start
  34.8 35.6 %reduce-scatter.4.cloned.1.call-done = f32[32,4608]{1,0:T(8,128)} async-done(((f32[128,4608]{1,0:T(8,128)}), f32[32,4608]{1,0:T(8,128)}) %reduce-scatter.4.cloned.1.call-update) | async-done | bytes 589840 | tf_op jit(solution)/shard_map/reduce_scatter | solution.py:25
  70.4 0.0 copy-done.3
  70.5 0.9 fusion.9
  71.4 0.0 copy-done.2
  71.4 1.1 fusion.6
  72.4 0.7 pad_maximum_fusion.3
  73.2 0.0 all-gather.3.cloned.1.call-update
  73.2 0.0 reduce-scatter.6.cloned.1.call-start
  73.3 17.5 %all-gather.3.cloned.1.call-done = bf16[128,4608]{1,0:T(8,128)(2,1)} async-done(((bf16[32,4608]{1,0:T(8,128)(2,1)}), bf16[128,4608]{1,0:T(8,128)(2,1)}) %all-gather.3.cloned.1.call-update) | async-done | bytes 1179664 | tf_op jit(solution)/shard_map/all_gather | solution.py:35
  90.8 4.8 %fusion.7 = f32[128,2048]{1,0:T(8,128)} fusion(bf16[2048,1024]{1,0:T(8,128)(2,1)} %param.11, bf16[128,4608]{1,0:T(8,128)(2,1)} %all-gather.3.cloned.1.call-done), kind=kOutput, calls=%fused_computation.12 | convolution fusion | flops 536870912 | bytes 5505024 | tf_op jit(solution)/shard_map/qc,fc->qf/dot_general | solution.py:39
  95.6 23.4 %fusion.2 = f32[128,7168]{1,0:T(8,128)} fusion(bf16[7168,3584]{1,0:T(8,128)(2,1)} %param.10, bf16[128,4608]{1,0:T(8,128)(2,1)} %all-gather.3.cloned.1.call-done), kind=kOutput, calls=%fused_computation.4 | convolution fusion | flops 6576668672 | bytes 55967744 | tf_op jit(solution)/shard_map/qc,fc->qf/dot_general | solution.py:36
  119.0 4.9 %pad_maximum_fusion = f32[128,9216]{1,0:T(8,128)} fusion(f32[128,2048]{1,0:T(8,128)} %fusion.7, f32[128,7168]{1,0:T(8,128)} %fusion.2), kind=kLoop, calls=%fused_computation | loop fusion | flops 1179648 | bytes 9437184 | tf_op jit(solution)/shard_map/concatenate | solution.py:42
  123.9 0.0 reduce-scatter.6.cloned.1.call-update
  124.0 0.0 all-gather.5.cloned.1.call-start
  124.0 95.8 %reduce-scatter.6.cloned.1.call-done = f32[16,9216]{1,0:T(8,128)} async-done(((f32[128,9216]{1,0:T(8,128)}), f32[16,9216]{1,0:T(8,128)}) %reduce-scatter.6.cloned.1.call-update) | async-done | bytes 589840 | tf_op jit(solution)/shard_map/reduce_scatter | solution.py:43
  219.8 1.8 convert_element_type.4
  221.6 0.0 all-gather.5.cloned.1.call-update
  221.6 0.0 reduce-scatter.8.cloned.1.call-start
  221.7 51.6 %all-gather.5.cloned.1.call-done = bf16[128,9216]{1,0:T(8,128)(2,1)} async-done(((bf16[16,9216]{1,0:T(8,128)(2,1)}), bf16[128,9216]{1,0:T(8,128)(2,1)}) %all-gather.5.cloned.1.call-update) | async-done | bytes 2359312 | tf_op jit(solution)/shard_map/all_gather | solution.py:46
  273.3 0.0 copy-done
  273.3 0.0 copy-start.1
  273.3 2.4 fusion.4
  275.7 0.0 copy-done.1
  275.7 7.9 %fusion = f32[128,768]{1,0:T(8,128)S(1)} fusion(bf16[768,7168]{1,0:T(8,128)(2,1)} %param.14, bf16[128,9216]{1,0:T(8,128)(2,1)S(1)} %copy-done.1), kind=kOutput, calls=%fused_computation.2 | convolution fusion | flops 1409286144 | bytes 13238272 | tf_op jit(solution)/shard_map/qf,tf->qt/dot_general | solution.py:48
  283.6 1.0 pad_maximum_fusion.2
  284.5 0.0 reduce-scatter.8.cloned.1.call-update
  284.6 21.9 %reduce-scatter.8.cloned.1.call-done = f32[32,1536]{1,0:T(8,128)} async-done(((f32[128,1536]{1,0:T(8,128)}), f32[32,1536]{1,0:T(8,128)}) %reduce-scatter.8.cloned.1.call-update) | async-done | bytes 196624 | tf_op jit(solution)/shard_map/reduce_scatter | solution.py:54
  306.4 1.0 fusion.10
  307.4 0.6 bitcast_reduce_fusion
Async XLA Ops:
  6.5 266.8 %copy-start = (bf16[768,2048]{1,0:T(8,128)(2,1)S(1)}, bf16[768,2048]{1,0:T(8,128)(2,1)}, u32[]{:S(2)}) copy-start(bf16[768,2048]{1,0:T(8,128)(2,1)} %param.15) | copy-start | bytes 9437188
  6.5 63.9 %reduce-scatter.4.cloned.1.call-start = ((), (), s32[]{:S(2)}) async-start(), calls=%async_computation.3 | async-start | bytes 2949120 | tf_op jit(solution)/shard_map/reduce_scatter | solution.py:25
  31.5 39.0 %copy-start.3 = (f32[1024]{0:T(1024)S(1)}, f32[1024]{0:T(1024)}, u32[]{:S(2)}) copy-start(f32[1024]{0:T(1024)} %param.13) | copy-start | bytes 12292
  31.5 39.9 %copy-start.2 = (f32[3584]{0:T(1024)S(1)}, f32[3584]{0:T(1024)}, u32[]{:S(2)}) copy-start(f32[3584]{0:T(1024)} %param.12) | copy-start | bytes 43012
  34.8 56.0 %all-gather.3.cloned.1.call-start = ((), (), s32[]{:S(2)}) async-start(), calls=%async_computation.4 | async-start | bytes 1474560 | tf_op jit(solution)/shard_map/all_gather | solution.py:35
  73.2 146.6 %reduce-scatter.6.cloned.1.call-start = ((), (), s32[]{:S(2)}) async-start(), calls=%async_computation.5 | async-start | bytes 5308416 | tf_op jit(solution)/shard_map/reduce_scatter | solution.py:43
  124.0 149.3 %all-gather.5.cloned.1.call-start = ((), (), s32[]{:S(2)}) async-start(), calls=%async_computation.6 | async-start | bytes 2654208 | tf_op jit(solution)/shard_map/all_gather | solution.py:46
  221.6 84.8 %reduce-scatter.8.cloned.1.call-start = ((), (), s32[]{:S(2)}) async-start(), calls=%async_computation.7 | async-start | bytes 983040 | tf_op jit(solution)/shard_map/reduce_scatter | solution.py:54
  273.3 2.4 copy-start.1
Sparse Core Ops, SparseCore 0:
  34.9 35.5 reduce-scatter.3
  73.3 17.4 all-gather.2
  124.1 95.6 reduce-scatter.5
  221.8 51.4 all-gather.4
  284.7 21.7 reduce-scatter.7
where the time goes:
time: 315 us
  waiting for transfers between devices  223 us (71%)
  matrix products  63.3 us (20%)
  other arithmetic  15.3 us (5%)
  between operations  13.2 us (4%)
    reduce_scatter x1, waiting for transfers between devices, per_device(): lax.psum_scatter(partial_value, 'dp', scatter_dimension=0, tiled=True)  95.8 us
    all_gather x1, waiting for transfers between devices, per_device(): directions = lax.all_gather(shared_part, 'dp', axis=0, tiled=True)  51.6 us
    reduce_scatter x1, waiting for transfers between devices, per_device(): lax.psum_scatter(jnp.concatenate([rot_in, rot_out], axis=1), 'mp', scatte...  35.6 us
    dot_general x1, matrix products, per_device(): jnp.einsum('qc,fc->qf', segment[:, :input_cols], basis_inputs, preferred_...  23.4 us
    reduce_scatter x1, waiting for transfers between devices, per_device(): lax.psum_scatter(jnp.concatenate([inner_in, inner_out], axis=1), 'mp', sc...  21.9 us
    dot_general x1, matrix products, per_device(): jnp.dot(query_inputs, basis_inputs, preferred_element_type=jnp.float32)  20.9 us
    all_gather x1, waiting for transfers between devices, per_device(): segment = lax.all_gather(scaled, 'mp', axis=0, tiled=True)  17.5 us
    dot_general x1, matrix products, per_device(): jnp.einsum('qf,tf->qt', directions[:, :feat_in], train_inputs, preferred_...  7.86 us
  transfers between devices with their start and end apart: 5, of which 5 were waited for; matrix products, arithmetic and copies ran while one was open for 0% of the time, Pallas kernels for 0%

commit v1 on v0

--- a/solution.py
+++ b/solution.py
@@ -43,7 +43,14 @@
     shared_part = lax.psum_scatter(partial_value, "dp", scatter_dimension=0, tiled=True).astype(
         jnp.bfloat16
     )
-    directions = lax.all_gather(shared_part, "dp", axis=0, tiled=True)
+    size = lax.axis_size("dp")
+    right = [(i, (i + 1) % size) for i in range(size)]
+    parts = [shared_part]
+    for reach in range(1, size):
+        parts = [lax.ppermute(parts[0], "dp", right), *parts]
+    whole = jnp.concatenate(parts, axis=0)
+    shift = (lax.axis_index("dp") + 1) * parts[-1].shape[0]
+    directions = jnp.roll(whole, shift, axis=0)
     train_count = train_inputs.shape[0]
     inner_in = jnp.einsum(
         "qf,tf->qt", directions[:, :feat_in], train_inputs, preferred_element_type=jnp.float32

time: 315 us -> 337 us (1.070)
  waiting for transfers between devices: 223 us -> 238 us
  local copies, waits for them, and re-layouts: 0.02 us -> 10.9 us
  other arithmetic: 15.3 us -> 11.6 us
    ppermute x0 -> x7, waiting for transfers between devices: none -> 68.3 us  [per_device(): parts = [lax.ppermute(parts[0], 'dp', right), *parts]]
    all_gather x1 -> x0, waiting for transfers between devices: 51.6 us -> none  [per_device(): directions = lax.all_gather(shared_part, 'dp', axis=0, tiled=True)]
    unnamed x8 -> x42, local copies, waits for them, and re-layouts: 0.02 us -> 10.9 us
  transfers between devices with their start and end apart: 5 -> 11, of which waited for: 5 -> 11; matrix products, arithmetic and copies ran while one was open for 0% -> 0% of each run, Pallas kernels for 0% -> 0%
where the time goes in v1:
time: 337 us; the launch traced here: 336 us
  waiting for transfers between devices  238 us (71%)
  matrix products  60.6 us (18%)
  between operations  13.4 us (4%)
  other arithmetic  11.6 us (3%)
  local copies, waits for them, and re-layouts  10.9 us (3%)
    reduce_scatter x1, waiting for transfers between devices, per_device(): lax.psum_scatter(partial_value, 'dp', scatter_dimension=0, tiled=True)  95.8 us
    ppermute x7, waiting for transfers between devices, per_device(): parts = [lax.ppermute(parts[0], 'dp', right), *parts]  68.3 us
    reduce_scatter x1, waiting for transfers between devices, per_device(): lax.psum_scatter(jnp.concatenate([rot_in, rot_out], axis=1), 'mp', scatte...  35.6 us
    dot_general x1, matrix products, per_device(): jnp.einsum('qc,fc->qf', segment[:, :input_cols], basis_inputs, preferred_...  23.3 us
    dot_general x1, matrix products, per_device(): jnp.dot(query_inputs, basis_inputs, preferred_element_type=jnp.float32)  21.1 us
    reduce_scatter x1, waiting for transfers between devices, per_device(): lax.psum_scatter(jnp.concatenate([inner_in, inner_out], axis=1), 'mp', sc...  20.6 us
    all_gather x1, waiting for transfers between devices, per_device(): segment = lax.all_gather(scaled, 'mp', axis=0, tiled=True)  17.5 us
    unnamed x42, local copies, waits for them, and re-layouts  10.9 us
  transfers between devices with their start and end apart: 11, of which 11 were waited for; matrix products, arithmetic and copies ran while one was open for 0% of the time, Pallas kernels for 0%

profile of v1, /device:TPU:0, one launch (start us, length us, event | category | flops | bytes accessed | tf_op | source)
XLA Modules:
  0.0 336.0 jit_solution(2107968502903033077)
XLA Ops:
  6.5 0.0 copy-start
  6.5 0.0 reduce-scatter.4.cloned.1.call-start
  6.5 21.1 %fusion.12 = f32[128,3584]{1,0:T(8,128)} fusion(bf16[128,7168]{1,0:T(8,128)(2,1)} %param.8, bf16[7168,3584]{1,0:T(8,128)(2,1)} %param.10), kind=kOutput, calls=%fused_computation.36 | convolution fusion | flops 6576668672 | bytes 55050240 | tf_op jit(solution)/shard_map/dot_general | solution.py:23
  27.6 3.2 fusion.13
  30.8 0.0 copy-done.2
  30.8 0.0 copy-start.12
  30.9 0.0 copy-start.13
  30.9 1.6 pad_maximum_fusion.1
  32.5 0.0 reduce-scatter.4.cloned.1.call-update
  32.5 0.0 all-gather.2.cloned.1.call-start
  32.5 35.6 %reduce-scatter.4.cloned.1.call-done = f32[32,4608]{1,0:T(8,128)} async-done(((f32[128,4608]{1,0:T(8,128)}), f32[32,4608]{1,0:T(8,128)}) %reduce-scatter.4.cloned.1.call-update) | async-done | bytes 589840 | tf_op jit(solution)/shard_map/reduce_scatter | solution.py:25
  68.2 0.0 copy-done.12
  68.2 1.1 fusion.6
  69.2 0.0 copy-done.13
  69.2 0.9 fusion.9
  70.2 0.7 pad_maximum_fusion.3
  70.9 0.0 all-gather.2.cloned.1.call-update
  70.9 0.0 reduce-scatter.6.cloned.1.call-start
  71.0 17.5 %all-gather.2.cloned.1.call-done = bf16[128,4608]{1,0:T(8,128)(2,1)} async-done(((bf16[32,4608]{1,0:T(8,128)(2,1)}), bf16[128,4608]{1,0:T(8,128)(2,1)}) %all-gather.2.cloned.1.call-update) | async-done | bytes 1179664 | tf_op jit(solution)/shard_map/all_gather | solution.py:35
  88.5 23.3 %fusion.2 = f32[128,7168]{1,0:T(8,128)} fusion(bf16[7168,3584]{1,0:T(8,128)(2,1)} %param.10, bf16[128,4608]{1,0:T(8,128)(2,1)} %all-gather.2.cloned.1.call-done), kind=kOutput, calls=%fused_computation.4 | convolution fusion | flops 6576668672 | bytes 55967744 | tf_op jit(solution)/shard_map/qc,fc->qf/dot_general | solution.py:36
  111.8 3.9 %fusion.7 = f32[128,2048]{1,0:T(8,128)S(1)} fusion(bf16[2048,1024]{1,0:T(8,128)(2,1)} %param.11, bf16[128,4608]{1,0:T(8,128)(2,1)} %all-gather.2.cloned.1.call-done), kind=kOutput, calls=%fused_computation.12 | convolution fusion | flops 536870912 | bytes 5505024 | tf_op jit(solution)/shard_map/qc,fc->qf/dot_general | solution.py:39
  115.8 0.0 copy-done.1
  115.8 2.5 pad_maximum_fusion
  118.3 0.0 reduce-scatter.6.cloned.1.call-update
  118.3 0.0 reduce-scatter.8.cloned.1.call-start
  118.3 95.8 %reduce-scatter.6.cloned.1.call-done = f32[16,9216]{1,0:T(8,128)} async-done(((f32[128,9216]{1,0:T(8,128)}), f32[16,9216]{1,0:T(8,128)}) %reduce-scatter.6.cloned.1.call-update) | async-done | bytes 589840 | tf_op jit(solution)/shard_map/reduce_scatter | solution.py:43
  214.1 1.1 convert_element_type.4
  215.2 1.5 collective-permute-start
  216.7 9.7 %collective-permute-done = bf16[16,9216]{1,0:T(8,128)(2,1)S(1)} collective-permute-done((bf16[16,9216]{1,0:T(8,128)(2,1)S(1)}, bf16[16,9216]{1,0:T(8,128)(2,1)S(1)}, u32[]{:S(2)}, u32[]{:S(2)}) %collective-permute-start) | collective-permute-done | bytes 294944 | tf_op jit(solution)/shard_map/ppermute | solution.py:50
  226.4 0.0 collective-permute-start.1
  226.4 10.3 %collective-permute-done.1 = bf16[16,9216]{1,0:T(8,128)(2,1)S(1)} collective-permute-done((bf16[16,9216]{1,0:T(8,128)(2,1)S(1)}, bf16[16,9216]{1,0:T(8,128)(2,1)S(1)}, u32[]{:S(2)}, u32[]{:S(2)}) %collective-permute-start.1) | collective-permute-done | bytes 294944 | tf_op jit(solution)/shard_map/ppermute | solution.py:50
  236.7 0.7 copy-done.4
  237.4 0.0 collective-permute-start.2
  237.4 9.4 %collective-permute-done.2 = bf16[16,9216]{1,0:T(8,128)(2,1)S(1)} collective-permute-done((bf16[16,9216]{1,0:T(8,128)(2,1)S(1)}, bf16[16,9216]{1,0:T(8,128)(2,1)S(1)}, u32[]{:S(2)}, u32[]{:S(2)}) %collective-permute-start.2) | collective-permute-done | bytes 294944 | tf_op jit(solution)/shard_map/ppermute | solution.py:50
  246.9 0.7 copy-done.6
  247.6 0.0 collective-permute-start.3
  247.6 9.4 %collective-permute-done.3 = bf16[16,9216]{1,0:T(8,128)(2,1)S(1)} collective-permute-done((bf16[16,9216]{1,0:T(8,128)(2,1)S(1)}, bf16[16,9216]{1,0:T(8,128)(2,1)S(1)}, u32[]{:S(2)}, u32[]{:S(2)}) %collective-permute-start.3) | collective-permute-done | bytes 294944 | tf_op jit(solution)/shard_map/ppermute | solution.py:50
  257.0 0.7 copy-done.8
  257.7 0.0 collective-permute-start.4
  257.7 9.4 %collective-permute-done.4 = bf16[16,9216]{1,0:T(8,128)(2,1)S(1)} collective-permute-done((bf16[16,9216]{1,0:T(8,128)(2,1)S(1)}, bf16[16,9216]{1,0:T(8,128)(2,1)S(1)}, u32[]{:S(2)}, u32[]{:S(2)}) %collective-permute-start.4) | collective-permute-done | bytes 294944 | tf_op jit(solution)/shard_map/ppermute | solution.py:50
  267.2 0.7 copy-done.10
  267.9 0.0 collective-permute-start.5
  267.9 10.4 %collective-permute-done.5 = bf16[16,9216]{1,0:T(8,128)(2,1)} collective-permute-done((bf16[16,9216]{1,0:T(8,128)(2,1)S(1)}, bf16[16,9216]{1,0:T(8,128)(2,1)}, u32[]{:S(2)}, u32[]{:S(2)}) %collective-permute-start.5) | collective-permute-done | bytes 294944 | tf_op jit(solution)/shard_map/ppermute | solution.py:50
  278.3 0.0 collective-permute-start.6
  278.3 0.0 copy-start.7
  278.3 9.7 %collective-permute-done.6 = bf16[16,9216]{1,0:T(8,128)(2,1)} collective-permute-done((bf16[16,9216]{1,0:T(8,128)(2,1)}, bf16[16,9216]{1,0:T(8,128)(2,1)}, u32[]{:S(2)}, u32[]{:S(2)}) %collective-permute-start.6) | collective-permute-done | bytes 294944 | tf_op jit(solution)/shard_map/ppermute | solution.py:50
  288.0 1.0 constant_dynamic-update-slice_fusion.15
  289.0 1.0 constant_dynamic-update-slice_fusion.14
  290.0 1.0 constant_dynamic-update-slice_fusion.13
  291.0 1.0 constant_dynamic-update-slice_fusion.12
  291.9 1.0 constant_dynamic-update-slice_fusion.11
  292.9 1.0 constant_dynamic-update-slice_fusion.10
  293.9 1.1 constant_dynamic-update-slice_fusion.8
  295.0 1.0 constant_dynamic-update-slice_fusion.7
  296.0 1.0 constant_dynamic-update-slice_fusion.6
  297.1 0.0 copy-done.7
  297.2 0.0 copy-done.3
  297.2 7.9 %fusion = f32[128,768]{1,0:T(8,128)S(1)} fusion(bf16[768,7168]{1,0:T(8,128)(2,1)} %param.14, bf16[256,9216]{1,0:T(8,128)(2,1)S(1)} %constant_dynamic-update-slice_fusion, s32[]{:T(128)S(6)} %select_n.14), kind=kOutput, calls=%fused_computation.2 | convolution fusion | flops 1409286144 | bytes 13238276 | tf_op jit(solution)/shard_map/qf,tf->qt/dot_general | solution.py:55
  305.1 1.2 fusion.4
  306.3 1.0 pad_maximum_fusion.2
  307.3 0.0 reduce-scatter.8.cloned.1.call-update
  307.3 20.6 %reduce-scatter.8.cloned.1.call-done = f32[32,1536]{1,0:T(8,128)} async-done(((f32[128,1536]{1,0:T(8,128)}), f32[32,1536]{1,0:T(8,128)}) %reduce-scatter.8.cloned.1.call-update) | async-done | bytes 196624 | tf_op jit(solution)/shard_map/reduce_scatter | solution.py:61
  327.9 1.0 fusion.10
  328.9 0.6 bitcast_reduce_fusion
  (21 shorter events, 0.2 us)
Async XLA Ops:
  6.5 298.6 %copy-start = (bf16[768,2048]{1,0:T(8,128)(2,1)S(1)}, bf16[768,2048]{1,0:T(8,128)(2,1)}, u32[]{:S(2)}) copy-start(bf16[768,2048]{1,0:T(8,128)(2,1)} %param.15) | copy-start | bytes 9437188
  6.5 61.6 %reduce-scatter.4.cloned.1.call-start = ((), (), s32[]{:S(2)}) async-start(), calls=%async_computation.3 | async-start | bytes 2949120 | tf_op jit(solution)/shard_map/reduce_scatter | solution.py:25
  27.6 3.2 copy-start.2
  30.8 37.3 %copy-start.12 = (f32[3584]{0:T(1024)S(1)}, f32[3584]{0:T(1024)}, u32[]{:S(2)}) copy-start(f32[3584]{0:T(1024)} %param.12) | copy-start | bytes 43012
  30.9 38.4 %copy-start.13 = (f32[1024]{0:T(1024)S(1)}, f32[1024]{0:T(1024)}, u32[]{:S(2)}) copy-start(f32[1024]{0:T(1024)} %param.13) | copy-start | bytes 12292
  32.5 56.0 %all-gather.2.cloned.1.call-start = ((), (), s32[]{:S(2)}) async-start(), calls=%async_computation.4 | async-start | bytes 1474560 | tf_op jit(solution)/shard_map/all_gather | solution.py:35
  70.9 143.2 %reduce-scatter.6.cloned.1.call-start = ((), (), s32[]{:S(2)}) async-start(), calls=%async_computation.5 | async-start | bytes 5308416 | tf_op jit(solution)/shard_map/reduce_scatter | solution.py:43
  111.8 3.9 %copy-start.1 = (f32[128,7168]{1,0:T(8,128)S(1)}, f32[128,7168]{1,0:T(8,128)}, u32[]{:S(2)}) copy-start(f32[128,7168]{1,0:T(8,128)} %fusion.2) | copy-start | bytes 11010052
  118.3 209.6 %reduce-scatter.8.cloned.1.call-start = ((), (), s32[]{:S(2)}) async-start(), calls=%async_computation.6 | async-start | bytes 983040 | tf_op jit(solution)/shard_map/reduce_scatter | solution.py:61
  215.2 11.2 %collective-permute-start = (bf16[16,9216]{1,0:T(8,128)(2,1)S(1)}, bf16[16,9216]{1,0:T(8,128)(2,1)S(1)}, u32[]{:S(2)}, u32[]{:S(2)}) collective-permute-start(bf16[16,9216]{1,0:T(8,128)(2,1)S(1)} %convert_element_type.4), channel_id=1, source_target_pairs={{0,4},{4,8},{8,12},{12,16},{16,20},{20,24},{24,28},{28,0},{1,5},{5... | collective-permute-start | bytes 884744 | tf_op jit(solution)/shard_map/ppermute | solution.py:50
  226.4 10.3 %collective-permute-start.1 = (bf16[16,9216]{1,0:T(8,128)(2,1)S(1)}, bf16[16,9216]{1,0:T(8,128)(2,1)S(1)}, u32[]{:S(2)}, u32[]{:S(2)}) collective-permute-start(bf16[16,9216]{1,0:T(8,128)(2,1)S(1)} %collective-permute-done), channel_id=1, source_target_pairs={{0,4},{4,8},{8,12},{12,16},{16,20},{20,24},{24,28},{28,0},{1,5},{5... | collective-permute-start | bytes 884744 | tf_op jit(solution)/shard_map/ppermute | solution.py:50
  236.7 0.7 copy-start.4
  237.4 9.4 %collective-permute-start.2 = (bf16[16,9216]{1,0:T(8,128)(2,1)S(1)}, bf16[16,9216]{1,0:T(8,128)(2,1)S(1)}, u32[]{:S(2)}, u32[]{:S(2)}) collective-permute-start(bf16[16,9216]{1,0:T(8,128)(2,1)S(1)} %collective-permute-done.1), channel_id=1, source_target_pairs={{0,4},{4,8},{8,12},{12,16},{16,20},{20,24},{24,28},{28,0},{1,5},{5... | collective-permute-start | bytes 884744 | tf_op jit(solution)/shard_map/ppermute | solution.py:50
  246.9 0.7 copy-start.6
  247.6 9.4 %collective-permute-start.3 = (bf16[16,9216]{1,0:T(8,128)(2,1)S(1)}, bf16[16,9216]{1,0:T(8,128)(2,1)S(1)}, u32[]{:S(2)}, u32[]{:S(2)}) collective-permute-start(bf16[16,9216]{1,0:T(8,128)(2,1)S(1)} %collective-permute-done.2), channel_id=1, source_target_pairs={{0,4},{4,8},{8,12},{12,16},{16,20},{20,24},{24,28},{28,0},{1,5},{5... | collective-permute-start | bytes 884744 | tf_op jit(solution)/shard_map/ppermute | solution.py:50
  257.0 0.7 copy-start.8
  257.7 9.4 %collective-permute-start.4 = (bf16[16,9216]{1,0:T(8,128)(2,1)S(1)}, bf16[16,9216]{1,0:T(8,128)(2,1)S(1)}, u32[]{:S(2)}, u32[]{:S(2)}) collective-permute-start(bf16[16,9216]{1,0:T(8,128)(2,1)S(1)} %collective-permute-done.3), channel_id=1, source_target_pairs={{0,4},{4,8},{8,12},{12,16},{16,20},{20,24},{24,28},{28,0},{1,5},{5... | collective-permute-start | bytes 884744 | tf_op jit(solution)/shard_map/ppermute | solution.py:50
  267.2 0.7 copy-start.10
  267.9 10.4 %collective-permute-start.5 = (bf16[16,9216]{1,0:T(8,128)(2,1)S(1)}, bf16[16,9216]{1,0:T(8,128)(2,1)}, u32[]{:S(2)}, u32[]{:S(2)}) collective-permute-start(bf16[16,9216]{1,0:T(8,128)(2,1)S(1)} %collective-permute-done.4), channel_id=1, source_target_pairs={{0,4},{4,8},{8,12},{12,16},{16,20},{20,24},{24,28},{28,0},{1,5},{5... | collective-permute-start | bytes 884744 | tf_op jit(solution)/shard_map/ppermute | solution.py:50
  278.3 9.7 %collective-permute-start.6 = (bf16[16,9216]{1,0:T(8,128)(2,1)}, bf16[16,9216]{1,0:T(8,128)(2,1)}, u32[]{:S(2)}, u32[]{:S(2)}) collective-permute-start(bf16[16,9216]{1,0:T(8,128)(2,1)} %collective-permute-done.5), channel_id=1, source_target_pairs={{0,4},{4,8},{8,12},{12,16},{16,20},{20,24},{24,28},{28,0},{1,5},{5... | collective-permute-start | bytes 884744 | tf_op jit(solution)/shard_map/ppermute | solution.py:50
  278.3 18.7 %copy-start.11 = (bf16[16,9216]{1,0:T(8,128)(2,1)S(1)}, bf16[16,9216]{1,0:T(8,128)(2,1)}, u32[]{:S(2)}) copy-start(bf16[16,9216]{1,0:T(8,128)(2,1)} %copy-done.10) | copy-start | bytes 884740
  278.3 18.8 %copy-start.9 = (bf16[16,9216]{1,0:T(8,128)(2,1)S(1)}, bf16[16,9216]{1,0:T(8,128)(2,1)}, u32[]{:S(2)}) copy-start(bf16[16,9216]{1,0:T(8,128)(2,1)} %copy-done.8) | copy-start | bytes 884740
  278.3 18.8 %copy-start.7 = (bf16[16,9216]{1,0:T(8,128)(2,1)S(1)}, bf16[16,9216]{1,0:T(8,128)(2,1)}, u32[]{:S(2)}) copy-start(bf16[16,9216]{1,0:T(8,128)(2,1)} %copy-done.6) | copy-start | bytes 884740
  278.3 18.9 %copy-start.5 = (bf16[16,9216]{1,0:T(8,128)(2,1)S(1)}, bf16[16,9216]{1,0:T(8,128)(2,1)}, u32[]{:S(2)}) copy-start(bf16[16,9216]{1,0:T(8,128)(2,1)} %copy-done.4) | copy-start | bytes 884740
  278.3 18.9 %copy-start.3 = (f32[16,9216]{1,0:T(8,128)S(1)}, f32[16,9216]{1,0:T(8,128)}, u32[]{:S(2)}) copy-start(f32[16,9216]{1,0:T(8,128)} %reduce-scatter.6.cloned.1.call-done) | copy-start | bytes 1769476
Sparse Core Ops, SparseCore 0:
  32.6 35.5 reduce-scatter.3
  71.0 17.4 all-gather.1
  118.4 95.6 reduce-scatter.5
  307.4 20.4 reduce-scatter.7
